TPU v7x, 256 devices: a whole 4x4x8 slice. The times are simulated.
256 devices in a mesh: ctx: 8 (over z_lo, core), dp: 8 (over z_hi, y), head: 4 (over x).
Axes of the slice: x: 4, y: 4, z: 8 (z_hi: 2, z_lo: 4; z = z_hi * 4 + z_lo), core: 2. Of those that a mesh axis runs over, the one named last changes fastest.
Arguments:
- queries: bfloat16 [32768, 8, 128], P(('dp', 'ctx'), 'head'), parts along dimension 0, may hold values from -40 to 40
- keys: bfloat16 [32768, 128], P(('dp', 'ctx')), parts along dimension 0, may hold values from -6 to 6
- values: bfloat16 [32768, 128], P(('dp', 'ctx')), parts along dimension 0, may hold values from -6 to 6
- output: bfloat16 [32768, 8, 128], P(('dp', 'ctx'), 'head'), parts along dimension 0, may hold values from -6 to 6
- output_grad: bfloat16 [32768, 8, 128], P(('dp', 'ctx'), 'head'), parts along dimension 0, may hold values from -6 to 6
- block_doc: int32 [256], P('dp'), parts along dimension 0, may hold values from 0 to 3, never falling along the last dimension, each value on 1 to 24 neighbouring positions
Outputs:
- query_grad: bfloat16 [32768, 8, 128], P(('dp', 'ctx'), 'head'), parts along dimension 0
- key_grad: bfloat16 [32768, 128], P(('dp', 'ctx', 'head')), parts along dimension 0
- value_grad: bfloat16 [32768, 128], P(('dp', 'ctx', 'head')), parts along dimension 0
There are 8 independent parts, one for each index of `dp`. A program takes and returns all parts, laid end to end along the dimension named above; each array names one. Nothing has to cross between parts.
Inputs may be any that keep to these rules, and one draw needn't show every extreme that they name: block_doc[b] is the document of tokens b * 128 to (b + 1) * 128 - 1; ids never fall; each of the 4 documents spans 1 to 24 blocks, and one spans exactly 24.
All inputs are finite; a program needn't handle non-finite values.
Results may differ from a plain program's by a relative error of at most 0.0049.
Values may be sent and summed in bfloat16 or wider, within the bound.
No kernel may reach another device: no remote copies, remote signals or barrier semaphores. Data moves between devices by JAX's collectives and lax.ppermute only.
A program may use at most 64 MiB of HBM per device.

v0:
```python
import math

import jax
import jax.numpy as jnp
from jax import lax
from jax.experimental import pallas as pl
from jax.experimental.pallas import tpu as pltpu
from jax.sharding import PartitionSpec as P


BLK = 128
TILE = 256
floor_score = -1.0e30
masked_score = -2.0e30

NT = (((1,), (1,)), ((), ()))


def tile_bounds(ctx, starts, back, key_tile, key_rows, query_tile, shard_rows):
    key_base = (ctx - 2 * back) * shard_rows + key_tile * key_rows
    partner = ctx + 1 - 2 * lax.rem(ctx, 2)
    shard = jnp.where(query_tile < 2, ctx, partner)
    query_base = shard * shard_rows + lax.rem(query_tile, 2) * TILE
    block = lax.div(query_base, BLK)
    first, last = starts[block], starts[block + 1]
    seen = (key_base <= query_base + TILE - 1) & (key_base + key_rows - 1 >= first)
    inside = (key_base + key_rows - 1 <= query_base) & (key_base >= last)
    return (key_base, query_base, first, last), seen, inside


def tile_mask(edge, offset, rows, width):
    key_base, query_base, first, last = edge
    key_pos = key_base + offset + lax.broadcasted_iota(jnp.int32, (rows, width), 0)
    lane = lax.rem(lax.broadcasted_iota(jnp.int32, (1, width), 1), TILE)
    query_pos = query_base + lane
    start = jnp.where(lane < BLK, first, last)
    return (key_pos <= query_pos) & (key_pos >= start)


def each_tile(ctx, starts, back, shard_rows, tiles, visit):
    def step(query_tile, carry):
        _, seen, inside = tile_bounds(ctx, starts, back, 0, shard_rows, query_tile, shard_rows)

        @pl.when(inside)
        def _():
            visit(query_tile, 0, shard_rows, None)

        @pl.when(seen & jnp.logical_not(inside))
        def _():
            def part(key_tile, carry):
                edge, seen, _ = tile_bounds(ctx, starts, back, key_tile, TILE, query_tile, shard_rows)

                @pl.when(seen)
                def _():
                    visit(query_tile, pl.multiple_of(key_tile * TILE, TILE), TILE, edge)

                return carry

            lax.fori_loop(0, shard_rows // TILE, part, 0)

        return carry

    @pl.when(ctx >= 2 * back)
    def _():
        lax.fori_loop(0, tiles, step, 0)


def stat_chunk(scale, ctx, starts, back, rows, key_ref, store, tops, sums):
    tiles, width = rows.shape[1], rows.shape[2]
    sub = 32

    def visit(query_tile, base, count, edge):
        top = tops[query_tile]
        total = sums[query_tile]
        scores = lax.dot_general(
            key_ref[pl.ds(base, count), :], rows[0, query_tile], NT, preferred_element_type=jnp.float32
        )
        for offset in range(0, count, sub):
            score = scores[offset : offset + sub] * scale
            if edge is not None:
                score = jnp.where(tile_mask(edge, offset, sub, width), score, masked_score)
            if store is not None:
                store[query_tile, pl.ds(base + offset, sub), :] = score
            score = score.reshape(sub // 8, 8, width)
            new = jnp.maximum(top, jnp.max(score, axis=0))
            total = total * jnp.exp2(top - new) + jnp.sum(jnp.exp2(score - new[None]), axis=0)
            top = new
        sums[query_tile] = total
        tops[query_tile] = top

    each_tile(ctx, starts, back, key_ref.shape[0], tiles, visit)


def near_stats_body(scale, info, starts, rows, key_ref, tops, sums):
    tops[...] = jnp.full(tops.shape, floor_score, jnp.float32)
    sums[...] = jnp.zeros(sums.shape, jnp.float32)
    stat_chunk(scale, info[0], starts, 0, rows, key_ref, None, tops, sums)


def far_stats_body(scale, backs, last, info, starts, rows, delta, tops_in, sums_in, *refs):
    count = len(backs)
    keys, store, outs = refs[:count], refs[count], refs[count + 1 :]
    tiles = rows.shape[1]
    tops, sums = outs[-2:]
    tops[...] = tops_in[...]
    sums[...] = sums_in[...]
    for slot, (back, key_ref) in enumerate(zip(backs, keys)):
        stat_chunk(scale, info[0], starts, back, rows, key_ref, store.at[slot], tops, sums)
    if last:
        out = outs[0]
        for tile in range(tiles):
            top = jnp.max(tops[tile], axis=0, keepdims=True)
            out[tile : tile + 1, :] = top
            out[tiles + tile : tiles + tile + 1, :] = jnp.sum(
                sums[tile] * jnp.exp2(tops[tile] - top), axis=0, keepdims=True
            )
        half = tiles // 2
        out[2 * tiles : 2 * tiles + half, :] = delta[...]


def grad_body(scale, inv_root, owners, backs, slots, carried, last, info, starts, rows, mine, other, *refs):
    refs = list(refs)
    keys = [refs.pop(0) for _ in backs]
    values = [refs.pop(0) for _ in backs]
    stores = [refs.pop(0).at[slot] if back else None for back, slot in zip(backs, slots)]
    query_in = refs.pop(0) if carried else None
    kept = refs.pop(0)
    sends = [refs.pop(0) for _ in range(owners - 1)]
    query_parts = [refs.pop(0) for _ in range(2)] if last else None
    query_out, logs, deltas, key_acc, value_acc = refs
    ctx, head = info[0], info[1]
    tiles, width = rows.shape[1], rows.shape[2]
    shard_rows, size = key_acc.shape
    half = tiles // 2
    query_out[...] = query_in[...] if carried else jnp.zeros(query_out.shape, jnp.float32)
    for tile in range(tiles):
        twin = (tile + half) % tiles
        top_a, top_b = mine[tile : tile + 1, :], other[twin : twin + 1, :]
        sum_a, sum_b = mine[tiles + tile : tiles + tile + 1, :], other[tiles + twin : tiles + twin + 1, :]
        top = jnp.maximum(top_a, top_b)
        total = sum_a * jnp.exp2(top_a - top) + sum_b * jnp.exp2(top_b - top)
        logs[tile] = top + jnp.log2(total)
        source = mine if tile < half else other
        at = 2 * tiles + tile % half
        deltas[tile] = source[at : at + 1, :]
    part = shard_rows // owners
    for slot, back in enumerate(backs):
        key_ref, value_ref, store = keys[slot], values[slot], stores[slot]
        key_acc[...] = jnp.zeros(key_acc.shape, jnp.float32)
        value_acc[...] = jnp.zeros(value_acc.shape, jnp.float32)

        def visit(query_tile, base, count, edge, key_ref=key_ref, value_ref=value_ref, store=store):
            query, grad = rows[0, query_tile], rows[1, query_tile]
            log_total, delta = logs[query_tile], deltas[query_tile]
            score_grads = []
            for offset in range(0, count, TILE):
                at = pl.ds(base + offset, TILE)
                prob_grad = lax.dot_general(value_ref[at, :], grad, NT, preferred_element_type=jnp.float32)
                if store is None:
                    score = lax.dot_general(key_ref[at, :], query, NT, preferred_element_type=jnp.float32) * scale
                    if edge is not None:
                        score = jnp.where(tile_mask(edge, offset, TILE, width), score, masked_score)
                else:
                    score = store[query_tile, at, :]
                prob = jnp.exp2(score - log_total)
                score_grad = (prob * (prob_grad - delta)).astype(jnp.bfloat16)
                value_acc[at, :] += jnp.dot(prob.astype(jnp.bfloat16), grad, preferred_element_type=jnp.float32)
                key_acc[at, :] += jnp.dot(score_grad, query, preferred_element_type=jnp.float32)
                score_grads.append(score_grad)
            score_grad = jnp.concatenate(score_grads, axis=0)
            query_out[query_tile] += lax.dot_general(
                key_ref[pl.ds(base, count), :],
                score_grad,
                (((0,), (0,)), ((), ())),
                preferred_element_type=jnp.float32,
            )

        each_tile(ctx, starts, back, shard_rows, tiles, visit)

        for turn in range(owners):
            at = pl.ds(pl.multiple_of(lax.rem(head + turn, owners) * part, part), part)
            out = sends[turn - 1] if turn else kept
            out[slot, :, :size] = (key_acc[at, :] * inv_root).astype(out.dtype)
            out[slot, :, size:] = value_acc[at, :].astype(out.dtype)
    if last:
        query_parts[0][...] = query_out[:half]
        query_parts[1][...] = query_out[half:]


def vmem(count):
    return [pl.BlockSpec(memory_space=pltpu.VMEM)] * count


def smem(count):
    return [pl.BlockSpec(memory_space=pltpu.SMEM)] * count


def limit(mib):
    return pltpu.CompilerParams(vmem_limit_bytes=mib << 20)


def local(queries, keys, values, output, output_grad, block_doc):
    shard_rows, heads, size = queries.shape
    cycle = lax.axis_size("ctx")
    owners = lax.axis_size("head")
    steps = cycle // 2
    ctx = lax.axis_index("ctx").astype(jnp.int32)
    head = lax.axis_index("head").astype(jnp.int32)
    inv_root = size ** (-0.5)
    scale = inv_root * math.log2(math.e)
    half = shard_rows // TILE
    tiles, width = 2 * half, heads * TILE
    part = shard_rows // owners
    twins = [(i, i ^ 1) for i in range(cycle)]

    def swap(array):
        return lax.ppermute(array, "ctx", twins)

    def shift(array, back):
        return lax.ppermute(array, "ctx", [(i, i + 2 * back) for i in range(cycle - 2 * back)])

    def unshift(array, back):
        return lax.ppermute(array, "ctx", [(i + 2 * back, i) for i in range(cycle - 2 * back)])

    def turned(array, turn):
        return lax.ppermute(array, "head", [(i, (i + turn) % owners) for i in range(owners)])

    key_parts = [keys]
    for back in range(1, steps):
        key_parts.append(shift(keys, back))

    def tiled(array):
        return array.reshape(half, TILE, heads, size).transpose(0, 2, 1, 3).reshape(half, width, size)

    own_rows = jnp.stack([tiled(queries), tiled(output_grad)])
    other_rows = swap(own_rows)
    rows = jnp.concatenate([own_rows, other_rows], axis=1)
    value_parts = [values]
    for back in range(1, steps):
        value_parts.append(shift(values, back))
    delta = jnp.sum(output_grad.astype(jnp.float32) * output.astype(jnp.float32), axis=-1)
    delta = delta.reshape(half, TILE, heads).transpose(0, 2, 1).reshape(half, width)
    starts = BLK * jnp.sum((block_doc[None, :] < block_doc[:, None]).astype(jnp.int32), axis=1)
    info = jnp.stack([ctx, head])

    def stored(count):
        return jax.ShapeDtypeStruct((count, tiles, shard_rows, width), jnp.float32)

    running = (jax.ShapeDtypeStruct((tiles, 8, width), jnp.float32),) * 2
    tops, sums = pl.pallas_call(
        lambda *refs: near_stats_body(scale, *refs),
        out_shape=running,
        in_specs=smem(2) + vmem(2),
        out_specs=tuple(vmem(2)),
        compiler_params=limit(12),
        name="near_stats",
    )(info, starts, rows, keys)

    def far_stats(backs, tops, sums, last):
        return pl.pallas_call(
            lambda *refs: far_stats_body(scale, backs, last, *refs),
            out_shape=(stored(len(backs)),)
            + ((jax.ShapeDtypeStruct((4 * tiles, width), jnp.float32),) if last else ())
            + running,
            in_specs=smem(2) + vmem(4 + len(backs)),
            out_specs=tuple(vmem(4 if last else 3)),
            compiler_params=limit(12),
        )(info, starts, rows, delta, tops, sums, *[key_parts[back] for back in backs])

    store_1, tops, sums = far_stats((1,), tops, sums, False)
    store_23, stats = far_stats((2, 3), tops, sums, True)[:2]
    stores = [(None, 0), (store_1, 0), (store_23, 0), (store_23, 1)]
    other = swap(stats)

    def grads(backs, query_in, last):
        carried = query_in is not None
        count = len(backs)
        ins = [key_parts[back] for back in backs] + [value_parts[back] for back in backs]
        ins = ins + [stores[back][0] for back in backs if back] + ([query_in] if carried else [])
        slots = [stores[back][1] for back in backs]
        whole_query = jax.ShapeDtypeStruct((tiles, size, width), jnp.float32)
        half_query = jax.ShapeDtypeStruct((half, size, width), jnp.float32)
        outs = (jax.ShapeDtypeStruct((count, part, 2 * size), jnp.float32),)
        outs = outs + (jax.ShapeDtypeStruct((count, part, 2 * size), jnp.bfloat16),) * (owners - 1)
        outs = outs + ((half_query,) * 2 if last else ()) + (whole_query,)
        return pl.pallas_call(
            lambda *refs: grad_body(scale, inv_root, owners, backs, slots, carried, last, *refs),
            out_shape=outs,
            in_specs=smem(2) + vmem(3 + len(ins)),
            out_specs=tuple(vmem(len(outs))),
            scratch_shapes=[pltpu.VMEM((tiles, 1, width), jnp.float32)] * 2
            + [pltpu.VMEM((shard_rows, size), jnp.float32)] * 2,
            input_output_aliases={4 + len(ins): len(outs) - 1} if carried else {},
            compiler_params=limit(16),
        )(info, starts, rows, stats, other, *ins)

    kept_0, *sends_0, query_acc = grads((0,), None, False)
    kept_a, *sends_a, query_acc = grads((3, 2), query_acc, False)
    kept_b, *sends_b, query_own, query_other, _ = grads((1,), query_acc, True)
    came_a, came_b = [], []
    for turn in range(1, owners):
        both = jnp.concatenate([sends_a[turn - 1], sends_0[turn - 1]], axis=0)
        came_a.append(turned(both, turn))
        came_b.append(turned(sends_b[turn - 1], turn))
    query_came = swap(query_other)
    query_sum = query_own + query_came
    query_grad = (query_sum * inv_root).reshape(half, size, heads, TILE).transpose(0, 3, 2, 1)
    query_grad = query_grad.reshape(shard_rows, heads, size).astype(jnp.bfloat16)

    total_a = kept_a + sum(came[:2].astype(jnp.float32) for came in came_a)
    low_3, low_2 = total_a[0].astype(jnp.bfloat16), total_a[1].astype(jnp.bfloat16)
    total = kept_0[0] + sum(came[2].astype(jnp.float32) for came in came_a)
    low_1 = (kept_b[0] + sum(came[0].astype(jnp.float32) for came in came_b)).astype(jnp.bfloat16)
    back_3 = unshift(low_3, 3)
    back_2 = unshift(low_2, 2)
    back_1 = unshift(low_1, 1)
    total, query_grad = lax.optimization_barrier((total, query_grad))
    total = total + back_3.astype(jnp.float32) + back_2.astype(jnp.float32) + back_1.astype(jnp.float32)
    total = total.astype(jnp.bfloat16)
    return query_grad, total[:, :size], total[:, size:]


def solution(mesh):
    placed = (
        P(("dp", "ctx"), "head", None),
        P(("dp", "ctx"), None),
        P(("dp", "ctx"), None),
        P(("dp", "ctx"), "head", None),
        P(("dp", "ctx"), "head", None),
        P("dp"),
    )
    return jax.shard_map(
        local,
        mesh=mesh,
        in_specs=placed,
        out_specs=(
            P(("dp", "ctx"), "head", None),
            P(("dp", "ctx", "head"), None),
            P(("dp", "ctx", "head"), None),
        ),
        check_vma=False,
    )
```

profile of v0, /device:TPU:16, one launch (start us, length us, event | category | flops | bytes accessed | tf_op | source)
XLA Modules:
  0.0 68.3 jit_solution(7936335367628376133)
XLA Ops:
  0.6 0.0 copy-start.1
  0.6 0.0 copy-start.2
  0.7 4.0 %collective-permute-start.1 = (bf16[512,128]{1,0:T(8,128)(2,1)}, bf16[512,128]{1,0:T(8,128)(2,1)S(1)}, u32[]{:S(2)}, u32[]{:S(2)}) collective-permute-start(bf16[512,128]{1,0:T(8,128)(2,1)} %refs_5_.1), channel_id=1, source_target_pairs={{0,64},{32,96},{64,128},{96,160},{128,192},{160,224},{1,65},{33,97... | collective-permute-start | bytes 393224 | tf_op jit(solution)/shard_map/ppermute | solution.py:220
  4.6 5.2 %collective-permute-start.2 = (bf16[512,128]{1,0:T(8,128)(2,1)}, bf16[512,128]{1,0:T(8,128)(2,1)S(1)}, u32[]{:S(2)}, u32[]{:S(2)}) collective-permute-start(bf16[512,128]{1,0:T(8,128)(2,1)} %refs_5_.1), channel_id=1, source_target_pairs={{0,128},{32,160},{64,192},{96,224},{1,129},{33,161},{65,193},{97,2... | collective-permute-start | bytes 393224 | tf_op jit(solution)/shard_map/ppermute | solution.py:220
  9.8 1.3 %collective-permute-start.3 = (bf16[512,128]{1,0:T(8,128)(2,1)}, bf16[512,128]{1,0:T(8,128)(2,1)S(1)}, u32[]{:S(2)}, u32[]{:S(2)}) collective-permute-start(bf16[512,128]{1,0:T(8,128)(2,1)} %refs_5_.1), channel_id=1, source_target_pairs={{0,192},{32,224},{1,193},{33,225},{2,194},{34,226},{3,195},{35,227... | collective-permute-start | bytes 393224 | tf_op jit(solution)/shard_map/ppermute | solution.py:220
  11.1 1.0 %copy.21 = bf16[2,256,2,128]{3,1,2,0:T(8,128)(2,1)S(1)} copy(bf16[2,256,2,128]{3,2,1,0:T(2,128)(2,1)} %bitcast.33) | data formatting | bytes 524288 | tf_op jit(solution)/shard_map/reshape | solution.py:233
  12.1 1.0 %copy.22 = bf16[2,256,2,128]{3,1,2,0:T(8,128)(2,1)S(1)} copy(bf16[2,256,2,128]{3,2,1,0:T(2,128)(2,1)} %bitcast.31) | data formatting | bytes 524288 | tf_op jit(solution)/shard_map/reshape | solution.py:233
  13.1 0.1 pad_maximum_fusion.1
  13.2 0.1 collective-permute-start
  13.3 1.3 %collective-permute-start.5 = (bf16[512,128]{1,0:T(8,128)(2,1)}, bf16[512,128]{1,0:T(8,128)(2,1)S(1)}, u32[]{:S(2)}, u32[]{:S(2)}) collective-permute-start(bf16[512,128]{1,0:T(8,128)(2,1)} %refs_6_.1), channel_id=1, source_target_pairs={{0,192},{32,224},{1,193},{33,225},{2,194},{34,226},{3,195},{35,227... | collective-permute-start | bytes 393224 | tf_op jit(solution)/shard_map/ppermute | solution.py:220
  14.6 1.7 %multiply_reduce_fusion = f32[512,2]{1,0:T(8,128)S(1)} fusion(bf16[512,2,128]{2,1,0:T(2,128)(2,1)} %param.9, bf16[512,2,128]{2,1,0:T(2,128)(2,1)} %param.10), kind=kLoop, calls=%fused_computation.3 | loop fusion | flops 523264 | bytes 528384 | tf_op jit(solution)/shard_map/reduce_sum | solution.py:241
  16.2 0.1 copy.23
  16.4 0.1 pad_add_fusion.refs_0_
  16.4 0.9 %convert_reduce_fusion = s32[32]{0:T(128)S(1)} fusion(s32[32]{0:T(128)} %param.11), kind=kLoop, calls=%fused_computation.14 | loop fusion | flops 3040 | bytes 256 | tf_op jit(solution)/shard_map/reduce_sum | solution.py:243
  17.4 0.0 collective-permute-done
  17.4 1.3 %collective-permute-start.6 = (bf16[512,128]{1,0:T(8,128)(2,1)}, bf16[512,128]{1,0:T(8,128)(2,1)S(1)}, u32[]{:S(2)}, u32[]{:S(2)}) collective-permute-start(bf16[512,128]{1,0:T(8,128)(2,1)} %refs_6_.1), channel_id=1, source_target_pairs={{0,128},{32,160},{64,192},{96,224},{1,129},{33,161},{65,193},{97,2... | collective-permute-start | bytes 393224 | tf_op jit(solution)/shard_map/ppermute | solution.py:220
  18.7 0.1 pad_maximum_fusion.refs_2_
  18.8 0.0 copy-start
  18.8 0.9 %copy-done = bf16[512,128]{1,0:T(8,128)(2,1)S(1)} copy-done((bf16[512,128]{1,0:T(8,128)(2,1)S(1)}, bf16[512,128]{1,0:T(8,128)(2,1)}, u32[]{:S(2)}) %copy-start) | copy-done | bytes 131096
  19.7 2.0 %near_stats.1 = (f32[4,8,512]{2,1,0:T(8,128)S(1)}, f32[4,8,512]{2,1,0:T(8,128)S(1)}) custom-call(s32[2]{0:T(128)S(1)} %pad_add_fusion.refs_0_, s32[32]{0:T(128)S(1)} %broadcast_multiply_fusion.refs_1_, bf16[2,4,512,128]{3,2,1,0:T(8,128)(2,1)S(1)} %pad_maximum_fusion.refs_2_, bf16[512,128]{1,0:T(8,128)(2,1)S(1)} %copy-done), custom_call_target="tpu_custom_call" | custom-call | tf_op jit(solution)/shard_map/near_stats/pallas_call | solution.py:250
  21.7 0.0 collective-permute-done.1.refs_6_.refs_5_
  21.8 0.6 shard_map.85
  22.3 0.0 collective-permute-done.2.refs_6_
  22.3 0.0 collective-permute-done.3.refs_7_.refs_5_
  22.3 1.2 %shard_map.86 = (f32[2,4,512,512]{3,2,1,0:T(8,128)S(1)}, f32[16,512]{1,0:T(8,128)S(1)}, f32[4,8,512]{2,1,0:T(8,128)}, f32[4,8,512]{2,1,0:T(8,128)}) custom-call(s32[2]{0:T(128)S(1)} %pad_add_fusion.refs_0_, s32[32]{0:T(128)S(1)} %broadcast_multiply_fusion.refs_1_, bf16[2,4,512,128]{3,2,1,0:T(8,128)(2,1)S(1)} %pad_maximum_fusion.refs_2_, ...), custom_call_target="tpu_custom_call" | custom-call | tf_op jit(solution)/shard_map/pallas_call | solution.py:260
  23.5 0.1 collective-permute-start.4
  23.7 0.0 copy-done.2
  23.7 3.8 %collective-permute-start.10 = (bf16[512,128]{1,0:T(8,128)(2,1)S(1)}, bf16[512,128]{1,0:T(8,128)(2,1)S(1)}, u32[]{:S(2)}, u32[]{:S(2)}) collective-permute-start(bf16[512,128]{1,0:T(8,128)(2,1)S(1)} %copy-done.2), channel_id=1, source_target_pairs={{0,64},{32,96},{64,128},{96,160},{128,192},{160,224},{1,65},{33,97... | collective-permute-start | bytes 393224 | tf_op jit(solution)/shard_map/ppermute | solution.py:220
  27.5 0.0 collective-permute-done.4.refs_4_
  27.5 0.0 copy-done.1
  27.5 3.3 %shard_map.87 = (f32[1,128,256]{2,1,0:T(8,128)S(1)}, bf16[1,128,256]{2,1,0:T(8,128)(2,1)S(1)}, bf16[1,128,256]{2,1,0:T(8,128)(2,1)S(1)}, bf16[1,128,256]{2,1,0:T(8,128)(2,1)S(1)}, f32[4,128,512]{2,1,0:T(8,128)S(1)}) custom-call(s32[2]{0:T(128)S(1)} %pad_add_fusion.refs_0_, s32[32]{0:T(128)S(1)} %broadcast_multiply_fusion.refs_1_, ...), custom_call_target="tpu_custom_call" | custom-call | tf_op jit(solution)/shard_map/pallas_call | solution.py:286
  30.8 0.0 collective-permute-done.5.refs_7_
  30.8 0.0 collective-permute-done.6.refs_8_
  30.9 0.9 %shard_map.88 = (f32[2,128,256]{2,1,0:T(8,128)S(1)}, bf16[2,128,256]{2,1,0:T(8,128)(2,1)S(1)}, bf16[2,128,256]{2,1,0:T(8,128)(2,1)S(1)}, bf16[2,128,256]{2,1,0:T(8,128)(2,1)S(1)}, f32[4,128,512]{2,1,0:T(8,128)S(1)}) custom-call(s32[2]{0:T(128)S(1)} %pad_add_fusion.refs_0_, s32[32]{0:T(128)S(1)} %broadcast_multiply_fusion.refs_1_, ...), custom_call_target="tpu_custom_call", output_to_operand_aliasing={{4}: (11, {})} | custom-call | tf_op jit(solution)/shard_map/pallas_call | solution.py:286
  31.7 1.6 %collective-permute-start.7 = (bf16[3,128,256]{2,1,0:T(8,128)(2,1)S(1)}, bf16[3,128,256]{2,1,0:T(8,128)(2,1)S(1)}, u32[]{:S(2)}, u32[]{:S(2)}) collective-permute-start(bf16[3,128,256]{2,1,0:T(8,128)(2,1)S(1)} %pad_maximum_fusion.2), channel_id=1, source_target_pairs={{0,1},{1,2},{2,3},{3,0},{4,5},{5,6},{6,7},{7,4},{8,9},{9,10},{10,1... | collective-permute-start | bytes 589832 | tf_op jit(solution)/shard_map/ppermute | solution.py:226
  33.3 2.8 %collective-permute-start.8 = (bf16[3,128,256]{2,1,0:T(8,128)(2,1)S(1)}, bf16[3,128,256]{2,1,0:T(8,128)(2,1)S(1)}, u32[]{:S(2)}, u32[]{:S(2)}) collective-permute-start(bf16[3,128,256]{2,1,0:T(8,128)(2,1)S(1)} %pad_maximum_fusion.3), channel_id=1, source_target_pairs={{0,2},{1,3},{2,0},{3,1},{4,6},{5,7},{6,4},{7,5},{8,10},{9,11},{10,... | collective-permute-start | bytes 589832 | tf_op jit(solution)/shard_map/ppermute | solution.py:226
  36.2 0.0 collective-permute-done.10.refs_6_
  36.2 0.8 %shard_map.89 = (f32[1,128,256]{2,1,0:T(8,128)S(1)}, bf16[1,128,256]{2,1,0:T(8,128)(2,1)S(1)}, bf16[1,128,256]{2,1,0:T(8,128)(2,1)S(1)}, bf16[1,128,256]{2,1,0:T...) custom-call(s32[2]{0:T(128)S(1)} %pad_add_fusion.refs_0_, ...), custom_call_target="tpu_custom_call", output_to_operand_aliasing={{6}: (8, {})} | custom-call | tf_op jit(solution)/shard_map/pallas_call | solution.py:286
  37.0 0.3 collective-permute-start.14
  37.3 2.9 %collective-permute-start.15 = (bf16[1,128,256]{2,1,0:T(8,128)(2,1)S(1)}, bf16[1,128,256]{2,1,0:T(8,128)(2,1)S(1)}, u32[]{:S(2)}, u32[]{:S(2)}) collective-permute-start(bf16[1,128,256]{2,1,0:T(8,128)(2,1)S(1)} %get-tuple-element.51), channel_id=1, source_target_pairs={{0,2},{1,3},{2,0},{3,1},{4,6},{5,7},{6,4},{7,5},{8,10},{9,11},{10,... | collective-permute-start | bytes 196616 | tf_op jit(solution)/shard_map/ppermute | solution.py:226
  40.2 0.5 collective-permute-start.16
  40.7 3.0 %collective-permute-done.14 = bf16[1,128,256]{2,1,0:T(8,128)(2,1)S(1)} collective-permute-done((bf16[1,128,256]{2,1,0:T(8,128)(2,1)S(1)}, bf16[1,128,256]{2,1,0:T(8,128)(2,1)S(1)}, u32[]{:S(2)}, u32[]{:S(2)}) %collective-permute-start.14) | collective-permute-done | bytes 65568 | tf_op jit(solution)/shard_map/ppermute | solution.py:226
  43.7 3.1 %collective-permute-start.9 = (bf16[3,128,256]{2,1,0:T(8,128)(2,1)S(1)}, bf16[3,128,256]{2,1,0:T(8,128)(2,1)S(1)}, u32[]{:S(2)}, u32[]{:S(2)}) collective-permute-start(bf16[3,128,256]{2,1,0:T(8,128)(2,1)S(1)} %pad_maximum_fusion.4), channel_id=1, source_target_pairs={{0,3},{1,0},{2,1},{3,2},{4,7},{5,4},{6,5},{7,6},{8,11},{9,8},{10,9... | collective-permute-start | bytes 589832 | tf_op jit(solution)/shard_map/ppermute | solution.py:226
  46.8 0.1 collective-permute-done.15
  47.0 0.0 collective-permute-start.11
  47.0 0.0 collective-permute-done.16
  47.0 1.3 %collective-permute-start.17 = (bf16[128,256]{1,0:T(8,128)(2,1)S(1)}, bf16[128,256]{1,0:T(8,128)(2,1)S(1)}, u32[]{:S(2)}, u32[]{:S(2)}) collective-permute-start(bf16[128,256]{1,0:T(8,128)(2,1)S(1)} %fusion), channel_id=1, source_target_pairs={{64,0},{96,32},{128,64},{160,96},{192,128},{224,160},{65,1},{97,33... | collective-permute-start | bytes 196616 | tf_op jit(solution)/shard_map/ppermute | solution.py:223
  48.3 0.0 collective-permute-done.7
  48.3 0.0 collective-permute-done.8
  48.3 1.7 %collective-permute-done.9 = bf16[3,128,256]{2,1,0:T(8,128)(2,1)S(1)} collective-permute-done((bf16[3,128,256]{2,1,0:T(8,128)(2,1)S(1)}, bf16[3,128,256]{2,1,0:T(8,128)(2,1)S(1)}, u32[]{:S(2)}, u32[]{:S(2)}) %collective-permute-start.9) | collective-permute-done | bytes 196640 | tf_op jit(solution)/shard_map/ppermute | solution.py:226
  50.0 0.1 add_convert_fusion
  50.1 1.3 %collective-permute-start.12 = (bf16[128,256]{1,0:T(8,128)(2,1)S(1)}, bf16[128,256]{1,0:T(8,128)(2,1)S(1)}, u32[]{:S(2)}, u32[]{:S(2)}) collective-permute-start(bf16[128,256]{1,0:T(8,128)(2,1)S(1)} %get-tuple-element.53), channel_id=1, source_target_pairs={{192,0},{224,32},{193,1},{225,33},{194,2},{226,34},{195,3},{227,35... | collective-permute-start | bytes 196616 | tf_op jit(solution)/shard_map/ppermute | solution.py:223
  51.4 1.3 %collective-permute-start.13 = (bf16[128,256]{1,0:T(8,128)(2,1)S(1)}, bf16[128,256]{1,0:T(8,128)(2,1)S(1)}, u32[]{:S(2)}, u32[]{:S(2)}) collective-permute-start(bf16[128,256]{1,0:T(8,128)(2,1)S(1)} %get-tuple-element.54), channel_id=1, source_target_pairs={{128,0},{160,32},{192,64},{224,96},{129,1},{161,33},{193,65},{225,... | collective-permute-start | bytes 196616 | tf_op jit(solution)/shard_map/ppermute | solution.py:223
  52.7 0.0 collective-permute-done.11
  52.7 0.1 multiply_convert_fusion
  52.9 0.1 convert_element_type.82
  52.9 1.0 %copy.24 = bf16[2,256,2,128]{3,2,1,0:T(2,128)(2,1)} copy(bf16[2,256,2,128]{1,2,3,0:T(2,128)(2,1)S(1)} %bitcast.32) | data formatting | bytes 524288 | tf_op jit(solution)/shard_map/convert_element_type | solution.py:308
  53.9 0.0 collective-permute-done.17
  53.9 12.3 %collective-permute-done.12 = bf16[128,256]{1,0:T(8,128)(2,1)S(1)} collective-permute-done((bf16[128,256]{1,0:T(8,128)(2,1)S(1)}, bf16[128,256]{1,0:T(8,128)(2,1)S(1)}, u32[]{:S(2)}, u32[]{:S(2)}) %collective-permute-start.12) | collective-permute-done | bytes 65568 | tf_op jit(solution)/shard_map/ppermute | solution.py:223
  66.2 1.4 %collective-permute-done.13 = bf16[128,256]{1,0:T(8,128)(2,1)S(1)} collective-permute-done((bf16[128,256]{1,0:T(8,128)(2,1)S(1)}, bf16[128,256]{1,0:T(8,128)(2,1)S(1)}, u32[]{:S(2)}, u32[]{:S(2)}) %collective-permute-start.13) | collective-permute-done | bytes 65568 | tf_op jit(solution)/shard_map/ppermute | solution.py:223
  67.7 0.6 fusion.1
  (9 shorter events, 0.2 us)
Async XLA Ops:
  0.6 26.9 %copy-start.1 = (bf16[512,128]{1,0:T(8,128)(2,1)S(1)}, bf16[512,128]{1,0:T(8,128)(2,1)}, u32[]{:S(2)}) copy-start(bf16[512,128]{1,0:T(8,128)(2,1)} %refs_5_.1) | copy-start | bytes 393220
  0.6 23.0 %copy-start.2 = (bf16[512,128]{1,0:T(8,128)(2,1)S(1)}, bf16[512,128]{1,0:T(8,128)(2,1)}, u32[]{:S(2)}) copy-start(bf16[512,128]{1,0:T(8,128)(2,1)} %refs_6_.1) | copy-start | bytes 393220
  0.7 21.1 %collective-permute-start.1 = (bf16[512,128]{1,0:T(8,128)(2,1)}, bf16[512,128]{1,0:T(8,128)(2,1)S(1)}, u32[]{:S(2)}, u32[]{:S(2)}) collective-permute-start(bf16[512,128]{1,0:T(8,128)(2,1)} %refs_5_.1), channel_id=1, source_target_pairs={{0,64},{32,96},{64,128},{96,160},{128,192},{160,224},{1,65},{33,97... | collective-permute-start | bytes 393224 | tf_op jit(solution)/shard_map/ppermute | solution.py:220
  4.6 17.7 %collective-permute-start.2 = (bf16[512,128]{1,0:T(8,128)(2,1)}, bf16[512,128]{1,0:T(8,128)(2,1)S(1)}, u32[]{:S(2)}, u32[]{:S(2)}) collective-permute-start(bf16[512,128]{1,0:T(8,128)(2,1)} %refs_5_.1), channel_id=1, source_target_pairs={{0,128},{32,160},{64,192},{96,224},{1,129},{33,161},{65,193},{97,2... | collective-permute-start | bytes 393224 | tf_op jit(solution)/shard_map/ppermute | solution.py:220
  9.8 12.5 %collective-permute-start.3 = (bf16[512,128]{1,0:T(8,128)(2,1)}, bf16[512,128]{1,0:T(8,128)(2,1)S(1)}, u32[]{:S(2)}, u32[]{:S(2)}) collective-permute-start(bf16[512,128]{1,0:T(8,128)(2,1)} %refs_5_.1), channel_id=1, source_target_pairs={{0,192},{32,224},{1,193},{33,225},{2,194},{34,226},{3,195},{35,227... | collective-permute-start | bytes 393224 | tf_op jit(solution)/shard_map/ppermute | solution.py:220
  13.2 4.2 %collective-permute-start = (bf16[2,2,512,128]{3,2,1,0:T(8,128)(2,1)S(1)}, bf16[2,2,512,128]{3,2,1,0:T(8,128)(2,1)S(1)}, u32[]{:S(2)}, u32[]{:S(2)}) collective-permute-start(bf16[2,2,512,128]{3,2,1,0:T(8,128)(2,1)S(1)} %pad_maximum_fusion.1), channel_id=1, source_target_pairs={{0,32},{32,0},{64,96},{96,64},{128,160},{160,128},{192,224},{224,1... | collective-permute-start | bytes 1572872 | tf_op jit(solution)/shard_map/ppermute | solution.py:217
  13.3 17.6 %collective-permute-start.5 = (bf16[512,128]{1,0:T(8,128)(2,1)}, bf16[512,128]{1,0:T(8,128)(2,1)S(1)}, u32[]{:S(2)}, u32[]{:S(2)}) collective-permute-start(bf16[512,128]{1,0:T(8,128)(2,1)} %refs_6_.1), channel_id=1, source_target_pairs={{0,192},{32,224},{1,193},{33,225},{2,194},{34,226},{3,195},{35,227... | collective-permute-start | bytes 393224 | tf_op jit(solution)/shard_map/ppermute | solution.py:220
  17.4 13.5 %collective-permute-start.6 = (bf16[512,128]{1,0:T(8,128)(2,1)}, bf16[512,128]{1,0:T(8,128)(2,1)S(1)}, u32[]{:S(2)}, u32[]{:S(2)}) collective-permute-start(bf16[512,128]{1,0:T(8,128)(2,1)} %refs_6_.1), channel_id=1, source_target_pairs={{0,128},{32,160},{64,192},{96,224},{1,129},{33,161},{65,193},{97,2... | collective-permute-start | bytes 393224 | tf_op jit(solution)/shard_map/ppermute | solution.py:220
  18.8 0.9 %copy-start = (bf16[512,128]{1,0:T(8,128)(2,1)S(1)}, bf16[512,128]{1,0:T(8,128)(2,1)}, u32[]{:S(2)}) copy-start(bf16[512,128]{1,0:T(8,128)(2,1)} %refs_5_.1) | copy-start | bytes 393220
  23.5 4.0 %collective-permute-start.4 = (f32[16,512]{1,0:T(8,128)S(1)}, f32[16,512]{1,0:T(8,128)S(1)}, u32[]{:S(2)}, u32[]{:S(2)}) collective-permute-start(f32[16,512]{1,0:T(8,128)S(1)} %get-tuple-element.32.refs_3_), channel_id=1, source_target_pairs={{0,32},{32,0},{64,96},{96,64},{128,160},{160,128},{192,224},{224,1... | collective-permute-start | bytes 98312 | tf_op jit(solution)/shard_map/ppermute | solution.py:217
  23.7 12.5 %collective-permute-start.10 = (bf16[512,128]{1,0:T(8,128)(2,1)S(1)}, bf16[512,128]{1,0:T(8,128)(2,1)S(1)}, u32[]{:S(2)}, u32[]{:S(2)}) collective-permute-start(bf16[512,128]{1,0:T(8,128)(2,1)S(1)} %copy-done.2), channel_id=1, source_target_pairs={{0,64},{32,96},{64,128},{96,160},{128,192},{160,224},{1,65},{33,97... | collective-permute-start | bytes 393224 | tf_op jit(solution)/shard_map/ppermute | solution.py:220
  31.7 16.6 %collective-permute-start.7 = (bf16[3,128,256]{2,1,0:T(8,128)(2,1)S(1)}, bf16[3,128,256]{2,1,0:T(8,128)(2,1)S(1)}, u32[]{:S(2)}, u32[]{:S(2)}) collective-permute-start(bf16[3,128,256]{2,1,0:T(8,128)(2,1)S(1)} %pad_maximum_fusion.2), channel_id=1, source_target_pairs={{0,1},{1,2},{2,3},{3,0},{4,5},{5,6},{6,7},{7,4},{8,9},{9,10},{10,1... | collective-permute-start | bytes 589832 | tf_op jit(solution)/shard_map/ppermute | solution.py:226
  33.3 15.0 %collective-permute-start.8 = (bf16[3,128,256]{2,1,0:T(8,128)(2,1)S(1)}, bf16[3,128,256]{2,1,0:T(8,128)(2,1)S(1)}, u32[]{:S(2)}, u32[]{:S(2)}) collective-permute-start(bf16[3,128,256]{2,1,0:T(8,128)(2,1)S(1)} %pad_maximum_fusion.3), channel_id=1, source_target_pairs={{0,2},{1,3},{2,0},{3,1},{4,6},{5,7},{6,4},{7,5},{8,10},{9,11},{10,... | collective-permute-start | bytes 589832 | tf_op jit(solution)/shard_map/ppermute | solution.py:226
  37.0 6.7 %collective-permute-start.14 = (bf16[1,128,256]{2,1,0:T(8,128)(2,1)S(1)}, bf16[1,128,256]{2,1,0:T(8,128)(2,1)S(1)}, u32[]{:S(2)}, u32[]{:S(2)}) collective-permute-start(bf16[1,128,256]{2,1,0:T(8,128)(2,1)S(1)} %get-tuple-element.50), channel_id=1, source_target_pairs={{0,1},{1,2},{2,3},{3,0},{4,5},{5,6},{6,7},{7,4},{8,9},{9,10},{10,1... | collective-permute-start | bytes 196616 | tf_op jit(solution)/shard_map/ppermute | solution.py:226
  37.3 9.7 %collective-permute-start.15 = (bf16[1,128,256]{2,1,0:T(8,128)(2,1)S(1)}, bf16[1,128,256]{2,1,0:T(8,128)(2,1)S(1)}, u32[]{:S(2)}, u32[]{:S(2)}) collective-permute-start(bf16[1,128,256]{2,1,0:T(8,128)(2,1)S(1)} %get-tuple-element.51), channel_id=1, source_target_pairs={{0,2},{1,3},{2,0},{3,1},{4,6},{5,7},{6,4},{7,5},{8,10},{9,11},{10,... | collective-permute-start | bytes 196616 | tf_op jit(solution)/shard_map/ppermute | solution.py:226
  40.2 6.8 %collective-permute-start.16 = (bf16[1,128,256]{2,1,0:T(8,128)(2,1)S(1)}, bf16[1,128,256]{2,1,0:T(8,128)(2,1)S(1)}, u32[]{:S(2)}, u32[]{:S(2)}) collective-permute-start(bf16[1,128,256]{2,1,0:T(8,128)(2,1)S(1)} %get-tuple-element.52), channel_id=1, source_target_pairs={{0,3},{1,0},{2,1},{3,2},{4,7},{5,4},{6,5},{7,6},{8,11},{9,8},{10,9... | collective-permute-start | bytes 196616 | tf_op jit(solution)/shard_map/ppermute | solution.py:226
  43.7 6.3 %collective-permute-start.9 = (bf16[3,128,256]{2,1,0:T(8,128)(2,1)S(1)}, bf16[3,128,256]{2,1,0:T(8,128)(2,1)S(1)}, u32[]{:S(2)}, u32[]{:S(2)}) collective-permute-start(bf16[3,128,256]{2,1,0:T(8,128)(2,1)S(1)} %pad_maximum_fusion.4), channel_id=1, source_target_pairs={{0,3},{1,0},{2,1},{3,2},{4,7},{5,4},{6,5},{7,6},{8,11},{9,8},{10,9... | collective-permute-start | bytes 589832 | tf_op jit(solution)/shard_map/ppermute | solution.py:226
  47.0 5.8 %collective-permute-start.11 = (f32[2,128,512]{2,1,0:T(8,128)S(1)}, f32[2,128,512]{2,1,0:T(8,128)S(1)}, u32[]{:S(2)}, u32[]{:S(2)}) collective-permute-start(f32[2,128,512]{2,1,0:T(8,128)S(1)} %get-tuple-element.45), channel_id=1, source_target_pairs={{0,32},{32,0},{64,96},{96,64},{128,160},{160,128},{192,224},{224,1... | collective-permute-start | bytes 1572872 | tf_op jit(solution)/shard_map/ppermute | solution.py:217
  47.0 6.9 %collective-permute-start.17 = (bf16[128,256]{1,0:T(8,128)(2,1)S(1)}, bf16[128,256]{1,0:T(8,128)(2,1)S(1)}, u32[]{:S(2)}, u32[]{:S(2)}) collective-permute-start(bf16[128,256]{1,0:T(8,128)(2,1)S(1)} %fusion), channel_id=1, source_target_pairs={{64,0},{96,32},{128,64},{160,96},{192,128},{224,160},{65,1},{97,33... | collective-permute-start | bytes 196616 | tf_op jit(solution)/shard_map/ppermute | solution.py:223
  50.1 16.2 %collective-permute-start.12 = (bf16[128,256]{1,0:T(8,128)(2,1)S(1)}, bf16[128,256]{1,0:T(8,128)(2,1)S(1)}, u32[]{:S(2)}, u32[]{:S(2)}) collective-permute-start(bf16[128,256]{1,0:T(8,128)(2,1)S(1)} %get-tuple-element.53), channel_id=1, source_target_pairs={{192,0},{224,32},{193,1},{225,33},{194,2},{226,34},{195,3},{227,35... | collective-permute-start | bytes 196616 | tf_op jit(solution)/shard_map/ppermute | solution.py:223
  51.4 16.3 %collective-permute-start.13 = (bf16[128,256]{1,0:T(8,128)(2,1)S(1)}, bf16[128,256]{1,0:T(8,128)(2,1)S(1)}, u32[]{:S(2)}, u32[]{:S(2)}) collective-permute-start(bf16[128,256]{1,0:T(8,128)(2,1)S(1)} %get-tuple-element.54), channel_id=1, source_target_pairs={{128,0},{160,32},{192,64},{224,96},{129,1},{161,33},{193,65},{225,... | collective-permute-start | bytes 196616 | tf_op jit(solution)/shard_map/ppermute | solution.py:223
where the time goes:
time: 68.7 us; the launch traced here: 68.3 us
  starting transfers between devices  32.2 us (47%)
  waiting for transfers between devices  18.6 us (27%)
  Pallas kernels  8.8 us (13%)
  local copies, waits for them, and re-layouts  4.68 us (7%)
  other arithmetic  3.18 us (5%)
  between operations  0.95 us (1%)
    ppermute x6, starting transfers between devices, shift(): lax.ppermute(array, 'ctx', [(i, i + 2 * back) for i in range(cycle - 2 *...  16.9 us
    ppermute x3, waiting for transfers between devices, unshift(): lax.ppermute(array, 'ctx', [(i + 2 * back, i) for i in range(cycle - 2 *...  13.7 us
    ppermute x6, starting transfers between devices, turned(): lax.ppermute(array, 'head', [(i, (i + turn) % owners) for i in range(owne...  11.2 us
    pallas_call x3, Pallas kernels, grads(): pl.pallas_call(lambda *refs: grad_body(scale, inv_root, owners, backs, sl...  5 us
    ppermute x6, waiting for transfers between devices, turned(): lax.ppermute(array, 'head', [(i, (i + turn) % owners) for i in range(owne...  4.79 us
    ppermute x3, starting transfers between devices, unshift(): lax.ppermute(array, 'ctx', [(i + 2 * back, i) for i in range(cycle - 2 *...  3.88 us
    pallas_call x1, Pallas kernels, local(): pl.pallas_call(lambda *refs: near_stats_body(scale, *refs), out_shape=run...  2.04 us
    reshape x2, local copies, waits for them, and re-layouts, tiled(): array.reshape(half, TILE, heads, size).transpose(0, 2, 1, 3)  1.97 us
  transfers between devices with their start and end apart: 18, of which 5 were waited for; matrix products, arithmetic and copies ran while one was open for 9% of the time, Pallas kernels for 13%

commit v1 on v0

--- a/solution.py
+++ b/solution.py
@@ -37,7 +37,7 @@
     return (key_pos <= query_pos) & (key_pos >= start)
 
 
-def each_tile(ctx, starts, back, shard_rows, tiles, visit):
+def each_tile(ctx, starts, back, shard_rows, first, last, visit):
     def step(query_tile, carry):
         _, seen, inside = tile_bounds(ctx, starts, back, 0, shard_rows, query_tile, shard_rows)
 
@@ -62,14 +62,14 @@
 
     @pl.when(ctx >= 2 * back)
     def _():
-        lax.fori_loop(0, tiles, step, 0)
+        lax.fori_loop(first, last, step, 0)
 
 
 def stat_chunk(scale, ctx, starts, back, rows, key_ref, store, tops, sums):
     tiles, width = rows.shape[1], rows.shape[2]
     sub = 32
 
-    def visit(query_tile, base, count, edge):
+    def visit(query_tile, base, count, edge, keep=True):
         top = tops[query_tile]
         total = sums[query_tile]
         scores = lax.dot_general(
@@ -79,7 +79,7 @@
             score = scores[offset : offset + sub] * scale
             if edge is not None:
                 score = jnp.where(tile_mask(edge, offset, sub, width), score, masked_score)
-            if store is not None:
+            if keep:
                 store[query_tile, pl.ds(base + offset, sub), :] = score
             score = score.reshape(sub // 8, 8, width)
             new = jnp.maximum(top, jnp.max(score, axis=0))
@@ -88,13 +88,22 @@
         sums[query_tile] = total
         tops[query_tile] = top
 
-    each_tile(ctx, starts, back, key_ref.shape[0], tiles, visit)
-
-
-def near_stats_body(scale, info, starts, rows, key_ref, tops, sums):
+    kept = store.shape[0]
+    each_tile(ctx, starts, back, key_ref.shape[0], 0, kept, visit)
+    if kept < tiles:
+        each_tile(ctx, starts, back, key_ref.shape[0], kept, tiles, lambda *args: visit(*args, keep=False))
+
+
+def near_stats_body(scale, info, docs, rows, delta, key_ref, starts, store, delta_out, tops, sums):
+    start = jnp.int32(0)
+    starts[0] = start
+    for block in range(1, docs.shape[0]):
+        start = jnp.where(docs[block] == docs[block - 1], start, block * BLK)
+        starts[block] = start
+    delta_out[...] = delta[...]
     tops[...] = jnp.full(tops.shape, floor_score, jnp.float32)
     sums[...] = jnp.zeros(sums.shape, jnp.float32)
-    stat_chunk(scale, info[0], starts, 0, rows, key_ref, None, tops, sums)
+    stat_chunk(scale, info[0], starts, 0, rows, key_ref, store.at[0], tops, sums)
 
 
 def far_stats_body(scale, backs, last, info, starts, rows, delta, tops_in, sums_in, *refs):
@@ -122,7 +131,7 @@
     refs = list(refs)
     keys = [refs.pop(0) for _ in backs]
     values = [refs.pop(0) for _ in backs]
-    stores = [refs.pop(0).at[slot] if back else None for back, slot in zip(backs, slots)]
+    stores = [refs.pop(0).at[slot] for slot in slots]
     query_in = refs.pop(0) if carried else None
     kept = refs.pop(0)
     sends = [refs.pop(0) for _ in range(owners - 1)]
@@ -149,14 +158,14 @@
         key_acc[...] = jnp.zeros(key_acc.shape, jnp.float32)
         value_acc[...] = jnp.zeros(value_acc.shape, jnp.float32)
 
-        def visit(query_tile, base, count, edge, key_ref=key_ref, value_ref=value_ref, store=store):
+        def visit(query_tile, base, count, edge, keep=True, key_ref=key_ref, value_ref=value_ref, store=store):
             query, grad = rows[0, query_tile], rows[1, query_tile]
             log_total, delta = logs[query_tile], deltas[query_tile]
             score_grads = []
             for offset in range(0, count, TILE):
                 at = pl.ds(base + offset, TILE)
                 prob_grad = lax.dot_general(value_ref[at, :], grad, NT, preferred_element_type=jnp.float32)
-                if store is None:
+                if not keep:
                     score = lax.dot_general(key_ref[at, :], query, NT, preferred_element_type=jnp.float32) * scale
                     if edge is not None:
                         score = jnp.where(tile_mask(edge, offset, TILE, width), score, masked_score)
@@ -175,7 +184,10 @@
                 preferred_element_type=jnp.float32,
             )
 
-        each_tile(ctx, starts, back, shard_rows, tiles, visit)
+        stored = store.shape[0]
+        each_tile(ctx, starts, back, shard_rows, 0, stored, visit)
+        if stored < tiles:
+            each_tile(ctx, starts, back, shard_rows, stored, tiles, lambda *args, visit=visit: visit(*args, keep=False))
 
         for turn in range(owners):
             at = pl.ds(pl.multiple_of(lax.rem(head + turn, owners) * part, part), part)
@@ -240,21 +252,20 @@
         value_parts.append(shift(values, back))
     delta = jnp.sum(output_grad.astype(jnp.float32) * output.astype(jnp.float32), axis=-1)
     delta = delta.reshape(half, TILE, heads).transpose(0, 2, 1).reshape(half, width)
-    starts = BLK * jnp.sum((block_doc[None, :] < block_doc[:, None]).astype(jnp.int32), axis=1)
     info = jnp.stack([ctx, head])
 
-    def stored(count):
-        return jax.ShapeDtypeStruct((count, tiles, shard_rows, width), jnp.float32)
+    def stored(count, kept=tiles):
+        return jax.ShapeDtypeStruct((count, kept, shard_rows, width), jnp.float32)
 
     running = (jax.ShapeDtypeStruct((tiles, 8, width), jnp.float32),) * 2
-    tops, sums = pl.pallas_call(
+    starts, store_0, delta, tops, sums = pl.pallas_call(
         lambda *refs: near_stats_body(scale, *refs),
-        out_shape=running,
-        in_specs=smem(2) + vmem(2),
-        out_specs=tuple(vmem(2)),
+        out_shape=(jax.ShapeDtypeStruct(block_doc.shape, jnp.int32), stored(1), jax.ShapeDtypeStruct(delta.shape, jnp.float32)) + running,
+        in_specs=smem(2) + vmem(3),
+        out_specs=tuple(smem(1) + vmem(4)),
         compiler_params=limit(12),
         name="near_stats",
-    )(info, starts, rows, keys)
+    )(info, block_doc, rows, delta, keys)
 
     def far_stats(backs, tops, sums, last):
         return pl.pallas_call(
@@ -269,14 +280,14 @@
 
     store_1, tops, sums = far_stats((1,), tops, sums, False)
     store_23, stats = far_stats((2, 3), tops, sums, True)[:2]
-    stores = [(None, 0), (store_1, 0), (store_23, 0), (store_23, 1)]
+    stores = [(store_0, 0), (store_1, 0), (store_23, 0), (store_23, 1)]
     other = swap(stats)
 
     def grads(backs, query_in, last):
         carried = query_in is not None
         count = len(backs)
         ins = [key_parts[back] for back in backs] + [value_parts[back] for back in backs]
-        ins = ins + [stores[back][0] for back in backs if back] + ([query_in] if carried else [])
+        ins = ins + [stores[back][0] for back in backs] + ([query_in] if carried else [])
         slots = [stores[back][1] for back in backs]
         whole_query = jax.ShapeDtypeStruct((tiles, size, width), jnp.float32)
         half_query = jax.ShapeDtypeStruct((half, size, width), jnp.float32)

time: 68.7 us -> 71.3 us (1.038)
  starting transfers between devices: 32.2 us -> 34.8 us
  waiting for transfers between devices: 18.6 us -> 20.5 us
  other arithmetic: 3.18 us -> 2.24 us
  local copies, waits for them, and re-layouts: 4.68 us -> 3.82 us
    ppermute x6, starting transfers between devices: 16.9 us -> 20.5 us  [shift(): lax.ppermute(array, 'ctx', [(i, i + 2 * back) for i in range(cycle - 2 *...]
    ppermute x6, waiting for transfers between devices: 4.79 us -> 6.33 us  [turned(): lax.ppermute(array, 'head', [(i, (i + turn) % owners) for i in range(owne...]
    reduce_sum x1 -> x0, other arithmetic: 0.92 us -> none  [local(): jnp.sum((block_doc[None, :] < block_doc[:, None]).astype(jnp.int32), axis=1)]
    unnamed x7, local copies, waits for them, and re-layouts: 0.92 us -> 0.02 us
    ppermute x6, starting transfers between devices: 11.2 us -> 10.4 us  [turned(): lax.ppermute(array, 'head', [(i, (i + turn) % owners) for i in range(owne...]
    pallas_call x3, Pallas kernels: 5 us -> 4.19 us  [grads(): pl.pallas_call(lambda *refs: grad_body(scale, inv_root, owners, backs, sl...]
  transfers between devices with their start and end apart: 18 -> 18, of which waited for: 5 -> 5; matrix products, arithmetic and copies ran while one was open for 9% -> 5% of each run, Pallas kernels for 13% -> 12%
where the time goes in v1:
time: 71.3 us; the launch traced here: 71 us
  starting transfers between devices  34.8 us (49%)
  waiting for transfers between devices  20.5 us (29%)
  Pallas kernels  8.64 us (12%)
  local copies, waits for them, and re-layouts  3.82 us (5%)
  other arithmetic  2.24 us (3%)
  between operations  0.96 us (1%)
    ppermute x6, starting transfers between devices, shift(): lax.ppermute(array, 'ctx', [(i, i + 2 * back) for i in range(cycle - 2 *...  20.5 us
    ppermute x3, waiting for transfers between devices, unshift(): lax.ppermute(array, 'ctx', [(i + 2 * back, i) for i in range(cycle - 2 *...  14.2 us
    ppermute x6, starting transfers between devices, turned(): lax.ppermute(array, 'head', [(i, (i + turn) % owners) for i in range(owne...  10.4 us
    ppermute x6, waiting for transfers between devices, turned(): lax.ppermute(array, 'head', [(i, (i + turn) % owners) for i in range(owne...  6.33 us
    pallas_call x3, Pallas kernels, grads(): pl.pallas_call(lambda *refs: grad_body(scale, inv_root, owners, backs, sl...  4.19 us
    ppermute x3, starting transfers between devices, unshift(): lax.ppermute(array, 'ctx', [(i + 2 * back, i) for i in range(cycle - 2 *...  3.88 us
    pallas_call x1, Pallas kernels, local(): pl.pallas_call(lambda *refs: near_stats_body(scale, *refs), out_shape=(ja...  2.67 us
    reshape x2, local copies, waits for them, and re-layouts, tiled(): array.reshape(half, TILE, heads, size).transpose(0, 2, 1, 3)  2.01 us
  transfers between devices with their start and end apart: 18, of which 5 were waited for; matrix products, arithmetic and copies ran while one was open for 5% of the time, Pallas kernels for 12%

profile of v1, /device:TPU:16, one launch (start us, length us, event | category | flops | bytes accessed | tf_op | source)
XLA Modules:
  0.0 71.0 jit_solution(17113889238913480709)
XLA Ops:
  0.6 0.0 copy-start
  0.6 0.0 copy-start.2
  0.7 1.0 %copy.17 = bf16[2,256,2,128]{3,1,2,0:T(8,128)(2,1)S(1)} copy(bf16[2,256,2,128]{3,2,1,0:T(2,128)(2,1)} %bitcast.32) | data formatting | bytes 524288 | tf_op jit(solution)/shard_map/reshape | solution.py:245
  1.7 1.0 %copy.18 = bf16[2,256,2,128]{3,1,2,0:T(8,128)(2,1)S(1)} copy(bf16[2,256,2,128]{3,2,1,0:T(2,128)(2,1)} %bitcast.30) | data formatting | bytes 524288 | tf_op jit(solution)/shard_map/reshape | solution.py:245
  2.7 0.0 copy-start.1
  2.7 0.1 pad_maximum_fusion.1
  2.7 0.1 collective-permute-start
  2.8 3.8 %collective-permute-start.1 = (bf16[512,128]{1,0:T(8,128)(2,1)}, bf16[512,128]{1,0:T(8,128)(2,1)S(1)}, u32[]{:S(2)}, u32[]{:S(2)}) collective-permute-start(bf16[512,128]{1,0:T(8,128)(2,1)} %refs_5_.1), channel_id=1, source_target_pairs={{0,64},{32,96},{64,128},{96,160},{128,192},{160,224},{1,65},{33,97... | collective-permute-start | bytes 393224 | tf_op jit(solution)/shard_map/ppermute | solution.py:232
  6.7 5.2 %collective-permute-start.2 = (bf16[512,128]{1,0:T(8,128)(2,1)}, bf16[512,128]{1,0:T(8,128)(2,1)S(1)}, u32[]{:S(2)}, u32[]{:S(2)}) collective-permute-start(bf16[512,128]{1,0:T(8,128)(2,1)} %refs_5_.1), channel_id=1, source_target_pairs={{0,128},{32,160},{64,192},{96,224},{1,129},{33,161},{65,193},{97,2... | collective-permute-start | bytes 393224 | tf_op jit(solution)/shard_map/ppermute | solution.py:232
  11.9 1.3 %collective-permute-start.3 = (bf16[512,128]{1,0:T(8,128)(2,1)}, bf16[512,128]{1,0:T(8,128)(2,1)S(1)}, u32[]{:S(2)}, u32[]{:S(2)}) collective-permute-start(bf16[512,128]{1,0:T(8,128)(2,1)} %refs_5_.1), channel_id=1, source_target_pairs={{0,192},{32,224},{1,193},{33,225},{2,194},{34,226},{3,195},{35,227... | collective-permute-start | bytes 393224 | tf_op jit(solution)/shard_map/ppermute | solution.py:232
  13.2 1.3 %collective-permute-start.5 = (bf16[512,128]{1,0:T(8,128)(2,1)}, bf16[512,128]{1,0:T(8,128)(2,1)S(1)}, u32[]{:S(2)}, u32[]{:S(2)}) collective-permute-start(bf16[512,128]{1,0:T(8,128)(2,1)} %refs_6_.1), channel_id=1, source_target_pairs={{0,192},{32,224},{1,193},{33,225},{2,194},{34,226},{3,195},{35,227... | collective-permute-start | bytes 393224 | tf_op jit(solution)/shard_map/ppermute | solution.py:232
  14.5 1.7 %multiply_reduce_fusion = f32[512,2]{1,0:T(8,128)S(1)} fusion(bf16[512,2,128]{2,1,0:T(2,128)(2,1)} %param.9, bf16[512,2,128]{2,1,0:T(2,128)(2,1)} %param.10), kind=kLoop, calls=%fused_computation.3 | loop fusion | flops 523264 | bytes 528384 | tf_op jit(solution)/shard_map/reduce_sum | solution.py:253
  16.2 0.1 copy.19
  16.3 0.1 pad_add_fusion.refs_0_
  16.3 0.0 collective-permute-done
  16.4 1.3 %collective-permute-start.6 = (bf16[512,128]{1,0:T(8,128)(2,1)}, bf16[512,128]{1,0:T(8,128)(2,1)S(1)}, u32[]{:S(2)}, u32[]{:S(2)}) collective-permute-start(bf16[512,128]{1,0:T(8,128)(2,1)} %refs_6_.1), channel_id=1, source_target_pairs={{0,128},{32,160},{64,192},{96,224},{1,129},{33,161},{65,193},{97,2... | collective-permute-start | bytes 393224 | tf_op jit(solution)/shard_map/ppermute | solution.py:232
  17.7 0.1 pad_maximum_fusion.refs_2_
  17.8 0.0 copy-done
  17.8 0.0 copy-done.2
  17.8 2.7 %near_stats.1 = (s32[32]{0:T(128)S(1)}, f32[1,4,512,512]{3,2,1,0:T(8,128)S(1)}, f32[2,512]{1,0:T(2,128)S(1)}, f32[4,8,512]{2,1,0:T(8,128)S(1)}, f32[4,8,512]{2,1,0:T(8,128)S(1)}) custom-call(s32[2]{0:T(128)S(1)} %pad_add_fusion.refs_0_, s32[32]{0:T(128)S(1)} %copy-done.2, bf16[2,4,512,128]{3,2,1,0:T(8,128)(2,1)S(1)} %pad_maximum_fusion.refs_2_, ...), custom_call_target="tpu_custom_call" | custom-call | tf_op jit(solution)/shard_map/near_stats/pallas_call | solution.py:261
  20.5 0.0 collective-permute-done.1.refs_6_.refs_5_
  20.5 0.6 shard_map.85
  21.0 0.0 collective-permute-done.2.refs_6_
  21.1 0.0 collective-permute-done.3.refs_7_.refs_5_
  21.1 1.2 %shard_map.86 = (f32[2,4,512,512]{3,2,1,0:T(8,128)S(1)}, f32[16,512]{1,0:T(8,128)S(1)}, f32[4,8,512]{2,1,0:T(8,128)}, f32[4,8,512]{2,1,0:T(8,128)}) custom-call(s32[2]{0:T(128)S(1)} %pad_add_fusion.refs_0_, s32[32]{0:T(128)S(1)} %get-tuple-element.31.refs_1_, bf16[2,4,512,128]{3,2,1,0:T(8,128)(2,1)S(1)} %pad_maximum_fusion.refs_2_, ...), custom_call_target="tpu_custom_call" | custom-call | tf_op jit(solution)/shard_map/pallas_call | solution.py:271
  22.3 0.0 collective-permute-start.4
  22.3 0.0 copy-done.1
  22.3 7.5 %collective-permute-start.10 = (bf16[512,128]{1,0:T(8,128)(2,1)S(1)}, bf16[512,128]{1,0:T(8,128)(2,1)S(1)}, u32[]{:S(2)}, u32[]{:S(2)}) collective-permute-start(bf16[512,128]{1,0:T(8,128)(2,1)S(1)} %copy-done.1), channel_id=1, source_target_pairs={{0,64},{32,96},{64,128},{96,160},{128,192},{160,224},{1,65},{33,97... | collective-permute-start | bytes 393224 | tf_op jit(solution)/shard_map/ppermute | solution.py:232
  29.8 0.0 collective-permute-done.4.refs_4_
  29.9 2.5 %shard_map.87 = (f32[1,128,256]{2,1,0:T(8,128)S(1)}, bf16[1,128,256]{2,1,0:T(8,128)(2,1)S(1)}, bf16[1,128,256]{2,1,0:T(8,128)(2,1)S(1)}, bf16[1,128,256]{2,1,0:T(8,128)(2,1)S(1)}, f32[4,128,512]{2,1,0:T(8,128)S(1)}) custom-call(s32[2]{0:T(128)S(1)} %pad_add_fusion.refs_0_, s32[32]{0:T(128)S(1)} %get-tuple-element.31.refs_1_, ...), custom_call_target="tpu_custom_call" | custom-call | tf_op jit(solution)/shard_map/pallas_call | solution.py:297
  32.4 0.0 collective-permute-done.5.refs_7_
  32.4 0.0 collective-permute-done.6.refs_8_
  32.4 0.9 %shard_map.88 = (f32[2,128,256]{2,1,0:T(8,128)S(1)}, bf16[2,128,256]{2,1,0:T(8,128)(2,1)S(1)}, bf16[2,128,256]{2,1,0:T(8,128)(2,1)S(1)}, bf16[2,128,256]{2,1,0:T(8,128)(2,1)S(1)}, f32[4,128,512]{2,1,0:T(8,128)S(1)}) custom-call(s32[2]{0:T(128)S(1)} %pad_add_fusion.refs_0_, s32[32]{0:T(128)S(1)} %get-tuple-element.31.refs_1_, ...), custom_call_target="tpu_custom_call", output_to_operand_aliasing={{4}: (11, {})} | custom-call | tf_op jit(solution)/shard_map/pallas_call | solution.py:297
  33.3 1.6 %collective-permute-start.7 = (bf16[3,128,256]{2,1,0:T(8,128)(2,1)S(1)}, bf16[3,128,256]{2,1,0:T(8,128)(2,1)S(1)}, u32[]{:S(2)}, u32[]{:S(2)}) collective-permute-start(bf16[3,128,256]{2,1,0:T(8,128)(2,1)S(1)} %pad_maximum_fusion.2), channel_id=1, source_target_pairs={{0,1},{1,2},{2,3},{3,0},{4,5},{5,6},{6,7},{7,4},{8,9},{9,10},{10,1... | collective-permute-start | bytes 589832 | tf_op jit(solution)/shard_map/ppermute | solution.py:238
  34.9 2.8 %collective-permute-start.8 = (bf16[3,128,256]{2,1,0:T(8,128)(2,1)S(1)}, bf16[3,128,256]{2,1,0:T(8,128)(2,1)S(1)}, u32[]{:S(2)}, u32[]{:S(2)}) collective-permute-start(bf16[3,128,256]{2,1,0:T(8,128)(2,1)S(1)} %pad_maximum_fusion.3), channel_id=1, source_target_pairs={{0,2},{1,3},{2,0},{3,1},{4,6},{5,7},{6,4},{7,5},{8,10},{9,11},{10,... | collective-permute-start | bytes 589832 | tf_op jit(solution)/shard_map/ppermute | solution.py:238
  37.7 0.0 collective-permute-done.10.refs_6_
  37.7 0.8 %shard_map.89 = (f32[1,128,256]{2,1,0:T(8,128)S(1)}, bf16[1,128,256]{2,1,0:T(8,128)(2,1)S(1)}, bf16[1,128,256]{2,1,0:T(8,128)(2,1)S(1)}, bf16[1,128,256]{2,1,0:T...) custom-call(s32[2]{0:T(128)S(1)} %pad_add_fusion.refs_0_, ...), custom_call_target="tpu_custom_call", output_to_operand_aliasing={{6}: (8, {})} | custom-call | tf_op jit(solution)/shard_map/pallas_call | solution.py:297
  38.5 0.1 collective-permute-start.14
  38.6 2.9 %collective-permute-start.15 = (bf16[1,128,256]{2,1,0:T(8,128)(2,1)S(1)}, bf16[1,128,256]{2,1,0:T(8,128)(2,1)S(1)}, u32[]{:S(2)}, u32[]{:S(2)}) collective-permute-start(bf16[1,128,256]{2,1,0:T(8,128)(2,1)S(1)} %get-tuple-element.57), channel_id=1, source_target_pairs={{0,2},{1,3},{2,0},{3,1},{4,6},{5,7},{6,4},{7,5},{8,10},{9,11},{10,... | collective-permute-start | bytes 196616 | tf_op jit(solution)/shard_map/ppermute | solution.py:238
  41.5 0.5 collective-permute-start.16
  42.1 4.5 %collective-permute-done.14 = bf16[1,128,256]{2,1,0:T(8,128)(2,1)S(1)} collective-permute-done((bf16[1,128,256]{2,1,0:T(8,128)(2,1)S(1)}, bf16[1,128,256]{2,1,0:T(8,128)(2,1)S(1)}, u32[]{:S(2)}, u32[]{:S(2)}) %collective-permute-start.14) | collective-permute-done | bytes 65568 | tf_op jit(solution)/shard_map/ppermute | solution.py:238
  46.6 2.5 %collective-permute-start.9 = (bf16[3,128,256]{2,1,0:T(8,128)(2,1)S(1)}, bf16[3,128,256]{2,1,0:T(8,128)(2,1)S(1)}, u32[]{:S(2)}, u32[]{:S(2)}) collective-permute-start(bf16[3,128,256]{2,1,0:T(8,128)(2,1)S(1)} %pad_maximum_fusion.4), channel_id=1, source_target_pairs={{0,3},{1,0},{2,1},{3,2},{4,7},{5,4},{6,5},{7,6},{8,11},{9,8},{10,9... | collective-permute-start | bytes 589832 | tf_op jit(solution)/shard_map/ppermute | solution.py:238
  49.1 0.1 collective-permute-done.15
  49.2 0.0 collective-permute-start.11
  49.2 0.0 collective-permute-done.16
  49.3 1.3 %collective-permute-start.17 = (bf16[128,256]{1,0:T(8,128)(2,1)S(1)}, bf16[128,256]{1,0:T(8,128)(2,1)S(1)}, u32[]{:S(2)}, u32[]{:S(2)}) collective-permute-start(bf16[128,256]{1,0:T(8,128)(2,1)S(1)} %fusion), channel_id=1, source_target_pairs={{64,0},{96,32},{128,64},{160,96},{192,128},{224,160},{65,1},{97,33... | collective-permute-start | bytes 196616 | tf_op jit(solution)/shard_map/ppermute | solution.py:235
  50.6 0.0 collective-permute-done.7
  50.6 0.0 collective-permute-done.8
  50.6 1.7 %collective-permute-done.9 = bf16[3,128,256]{2,1,0:T(8,128)(2,1)S(1)} collective-permute-done((bf16[3,128,256]{2,1,0:T(8,128)(2,1)S(1)}, bf16[3,128,256]{2,1,0:T(8,128)(2,1)S(1)}, u32[]{:S(2)}, u32[]{:S(2)}) %collective-permute-start.9) | collective-permute-done | bytes 196640 | tf_op jit(solution)/shard_map/ppermute | solution.py:238
  52.3 0.1 add_convert_fusion
  52.3 1.3 %collective-permute-start.12 = (bf16[128,256]{1,0:T(8,128)(2,1)S(1)}, bf16[128,256]{1,0:T(8,128)(2,1)S(1)}, u32[]{:S(2)}, u32[]{:S(2)}) collective-permute-start(bf16[128,256]{1,0:T(8,128)(2,1)S(1)} %get-tuple-element.59), channel_id=1, source_target_pairs={{192,0},{224,32},{193,1},{225,33},{194,2},{226,34},{195,3},{227,35... | collective-permute-start | bytes 196616 | tf_op jit(solution)/shard_map/ppermute | solution.py:235
  53.6 1.3 %collective-permute-start.13 = (bf16[128,256]{1,0:T(8,128)(2,1)S(1)}, bf16[128,256]{1,0:T(8,128)(2,1)S(1)}, u32[]{:S(2)}, u32[]{:S(2)}) collective-permute-start(bf16[128,256]{1,0:T(8,128)(2,1)S(1)} %get-tuple-element.60), channel_id=1, source_target_pairs={{128,0},{160,32},{192,64},{224,96},{129,1},{161,33},{193,65},{225,... | collective-permute-start | bytes 196616 | tf_op jit(solution)/shard_map/ppermute | solution.py:235
  55.0 0.0 collective-permute-done.11
  55.0 0.1 multiply_convert_fusion
  55.1 0.1 convert_element_type.78
  55.2 1.0 %copy.20 = bf16[2,256,2,128]{3,2,1,0:T(2,128)(2,1)} copy(bf16[2,256,2,128]{1,2,3,0:T(2,128)(2,1)S(1)} %bitcast.31) | data formatting | bytes 524288 | tf_op jit(solution)/shard_map/convert_element_type | solution.py:319
  56.2 0.0 collective-permute-done.17
  56.2 12.8 %collective-permute-done.12 = bf16[128,256]{1,0:T(8,128)(2,1)S(1)} collective-permute-done((bf16[128,256]{1,0:T(8,128)(2,1)S(1)}, bf16[128,256]{1,0:T(8,128)(2,1)S(1)}, u32[]{:S(2)}, u32[]{:S(2)}) %collective-permute-start.12) | collective-permute-done | bytes 65568 | tf_op jit(solution)/shard_map/ppermute | solution.py:235
  68.9 1.4 %collective-permute-done.13 = bf16[128,256]{1,0:T(8,128)(2,1)S(1)} collective-permute-done((bf16[128,256]{1,0:T(8,128)(2,1)S(1)}, bf16[128,256]{1,0:T(8,128)(2,1)S(1)}, u32[]{:S(2)}, u32[]{:S(2)}) %collective-permute-start.13) | collective-permute-done | bytes 65568 | tf_op jit(solution)/shard_map/ppermute | solution.py:235
  70.4 0.6 fusion.1
  (8 shorter events, 0.2 us)
Async XLA Ops:
  0.6 17.1 %copy-start = (bf16[512,128]{1,0:T(8,128)(2,1)S(1)}, bf16[512,128]{1,0:T(8,128)(2,1)}, u32[]{:S(2)}) copy-start(bf16[512,128]{1,0:T(8,128)(2,1)} %refs_5_.1) | copy-start | bytes 393220
  0.6 17.1 %copy-start.2 = (s32[32]{0:T(128)S(1)}, s32[32]{0:T(128)}, u32[]{:S(2)}) copy-start(s32[32]{0:T(128)} %refs_1_.1) | copy-start | bytes 388
  2.7 19.6 %copy-start.1 = (bf16[512,128]{1,0:T(8,128)(2,1)S(1)}, bf16[512,128]{1,0:T(8,128)(2,1)}, u32[]{:S(2)}) copy-start(bf16[512,128]{1,0:T(8,128)(2,1)} %refs_6_.1) | copy-start | bytes 393220
  2.7 13.6 %collective-permute-start = (bf16[2,2,512,128]{3,2,1,0:T(8,128)(2,1)S(1)}, bf16[2,2,512,128]{3,2,1,0:T(8,128)(2,1)S(1)}, u32[]{:S(2)}, u32[]{:S(2)}) collective-permute-start(bf16[2,2,512,128]{3,2,1,0:T(8,128)(2,1)S(1)} %pad_maximum_fusion.1), channel_id=1, source_target_pairs={{0,32},{32,0},{64,96},{96,64},{128,160},{160,128},{192,224},{224,1... | collective-permute-start | bytes 1572872 | tf_op jit(solution)/shard_map/ppermute | solution.py:229
  2.8 17.6 %collective-permute-start.1 = (bf16[512,128]{1,0:T(8,128)(2,1)}, bf16[512,128]{1,0:T(8,128)(2,1)S(1)}, u32[]{:S(2)}, u32[]{:S(2)}) collective-permute-start(bf16[512,128]{1,0:T(8,128)(2,1)} %refs_5_.1), channel_id=1, source_target_pairs={{0,64},{32,96},{64,128},{96,160},{128,192},{160,224},{1,65},{33,97... | collective-permute-start | bytes 393224 | tf_op jit(solution)/shard_map/ppermute | solution.py:232
  6.7 14.4 %collective-permute-start.2 = (bf16[512,128]{1,0:T(8,128)(2,1)}, bf16[512,128]{1,0:T(8,128)(2,1)S(1)}, u32[]{:S(2)}, u32[]{:S(2)}) collective-permute-start(bf16[512,128]{1,0:T(8,128)(2,1)} %refs_5_.1), channel_id=1, source_target_pairs={{0,128},{32,160},{64,192},{96,224},{1,129},{33,161},{65,193},{97,2... | collective-permute-start | bytes 393224 | tf_op jit(solution)/shard_map/ppermute | solution.py:232
  11.9 9.2 %collective-permute-start.3 = (bf16[512,128]{1,0:T(8,128)(2,1)}, bf16[512,128]{1,0:T(8,128)(2,1)S(1)}, u32[]{:S(2)}, u32[]{:S(2)}) collective-permute-start(bf16[512,128]{1,0:T(8,128)(2,1)} %refs_5_.1), channel_id=1, source_target_pairs={{0,192},{32,224},{1,193},{33,225},{2,194},{34,226},{3,195},{35,227... | collective-permute-start | bytes 393224 | tf_op jit(solution)/shard_map/ppermute | solution.py:232
  13.2 19.2 %collective-permute-start.5 = (bf16[512,128]{1,0:T(8,128)(2,1)}, bf16[512,128]{1,0:T(8,128)(2,1)S(1)}, u32[]{:S(2)}, u32[]{:S(2)}) collective-permute-start(bf16[512,128]{1,0:T(8,128)(2,1)} %refs_6_.1), channel_id=1, source_target_pairs={{0,192},{32,224},{1,193},{33,225},{2,194},{34,226},{3,195},{35,227... | collective-permute-start | bytes 393224 | tf_op jit(solution)/shard_map/ppermute | solution.py:232
  16.4 16.0 %collective-permute-start.6 = (bf16[512,128]{1,0:T(8,128)(2,1)}, bf16[512,128]{1,0:T(8,128)(2,1)S(1)}, u32[]{:S(2)}, u32[]{:S(2)}) collective-permute-start(bf16[512,128]{1,0:T(8,128)(2,1)} %refs_6_.1), channel_id=1, source_target_pairs={{0,128},{32,160},{64,192},{96,224},{1,129},{33,161},{65,193},{97,2... | collective-permute-start | bytes 393224 | tf_op jit(solution)/shard_map/ppermute | solution.py:232
  22.3 7.6 %collective-permute-start.4 = (f32[16,512]{1,0:T(8,128)S(1)}, f32[16,512]{1,0:T(8,128)S(1)}, u32[]{:S(2)}, u32[]{:S(2)}) collective-permute-start(f32[16,512]{1,0:T(8,128)S(1)} %get-tuple-element.37.refs_3_), channel_id=1, source_target_pairs={{0,32},{32,0},{64,96},{96,64},{128,160},{160,128},{192,224},{224,1... | collective-permute-start | bytes 98312 | tf_op jit(solution)/shard_map/ppermute | solution.py:229
  22.3 15.4 %collective-permute-start.10 = (bf16[512,128]{1,0:T(8,128)(2,1)S(1)}, bf16[512,128]{1,0:T(8,128)(2,1)S(1)}, u32[]{:S(2)}, u32[]{:S(2)}) collective-permute-start(bf16[512,128]{1,0:T(8,128)(2,1)S(1)} %copy-done.1), channel_id=1, source_target_pairs={{0,64},{32,96},{64,128},{96,160},{128,192},{160,224},{1,65},{33,97... | collective-permute-start | bytes 393224 | tf_op jit(solution)/shard_map/ppermute | solution.py:232
  33.3 17.3 %collective-permute-start.7 = (bf16[3,128,256]{2,1,0:T(8,128)(2,1)S(1)}, bf16[3,128,256]{2,1,0:T(8,128)(2,1)S(1)}, u32[]{:S(2)}, u32[]{:S(2)}) collective-permute-start(bf16[3,128,256]{2,1,0:T(8,128)(2,1)S(1)} %pad_maximum_fusion.2), channel_id=1, source_target_pairs={{0,1},{1,2},{2,3},{3,0},{4,5},{5,6},{6,7},{7,4},{8,9},{9,10},{10,1... | collective-permute-start | bytes 589832 | tf_op jit(solution)/shard_map/ppermute | solution.py:238
  34.9 15.7 %collective-permute-start.8 = (bf16[3,128,256]{2,1,0:T(8,128)(2,1)S(1)}, bf16[3,128,256]{2,1,0:T(8,128)(2,1)S(1)}, u32[]{:S(2)}, u32[]{:S(2)}) collective-permute-start(bf16[3,128,256]{2,1,0:T(8,128)(2,1)S(1)} %pad_maximum_fusion.3), channel_id=1, source_target_pairs={{0,2},{1,3},{2,0},{3,1},{4,6},{5,7},{6,4},{7,5},{8,10},{9,11},{10,... | collective-permute-start | bytes 589832 | tf_op jit(solution)/shard_map/ppermute | solution.py:238
  38.5 8.0 %collective-permute-start.14 = (bf16[1,128,256]{2,1,0:T(8,128)(2,1)S(1)}, bf16[1,128,256]{2,1,0:T(8,128)(2,1)S(1)}, u32[]{:S(2)}, u32[]{:S(2)}) collective-permute-start(bf16[1,128,256]{2,1,0:T(8,128)(2,1)S(1)} %get-tuple-element.56), channel_id=1, source_target_pairs={{0,1},{1,2},{2,3},{3,0},{4,5},{5,6},{6,7},{7,4},{8,9},{9,10},{10,1... | collective-permute-start | bytes 196616 | tf_op jit(solution)/shard_map/ppermute | solution.py:238
  38.6 10.6 %collective-permute-start.15 = (bf16[1,128,256]{2,1,0:T(8,128)(2,1)S(1)}, bf16[1,128,256]{2,1,0:T(8,128)(2,1)S(1)}, u32[]{:S(2)}, u32[]{:S(2)}) collective-permute-start(bf16[1,128,256]{2,1,0:T(8,128)(2,1)S(1)} %get-tuple-element.57), channel_id=1, source_target_pairs={{0,2},{1,3},{2,0},{3,1},{4,6},{5,7},{6,4},{7,5},{8,10},{9,11},{10,... | collective-permute-start | bytes 196616 | tf_op jit(solution)/shard_map/ppermute | solution.py:238
  41.5 7.7 %collective-permute-start.16 = (bf16[1,128,256]{2,1,0:T(8,128)(2,1)S(1)}, bf16[1,128,256]{2,1,0:T(8,128)(2,1)S(1)}, u32[]{:S(2)}, u32[]{:S(2)}) collective-permute-start(bf16[1,128,256]{2,1,0:T(8,128)(2,1)S(1)} %get-tuple-element.58), channel_id=1, source_target_pairs={{0,3},{1,0},{2,1},{3,2},{4,7},{5,4},{6,5},{7,6},{8,11},{9,8},{10,9... | collective-permute-start | bytes 196616 | tf_op jit(solution)/shard_map/ppermute | solution.py:238
  46.6 5.7 %collective-permute-start.9 = (bf16[3,128,256]{2,1,0:T(8,128)(2,1)S(1)}, bf16[3,128,256]{2,1,0:T(8,128)(2,1)S(1)}, u32[]{:S(2)}, u32[]{:S(2)}) collective-permute-start(bf16[3,128,256]{2,1,0:T(8,128)(2,1)S(1)} %pad_maximum_fusion.4), channel_id=1, source_target_pairs={{0,3},{1,0},{2,1},{3,2},{4,7},{5,4},{6,5},{7,6},{8,11},{9,8},{10,9... | collective-permute-start | bytes 589832 | tf_op jit(solution)/shard_map/ppermute | solution.py:238
  49.2 5.8 %collective-permute-start.11 = (f32[2,128,512]{2,1,0:T(8,128)S(1)}, f32[2,128,512]{2,1,0:T(8,128)S(1)}, u32[]{:S(2)}, u32[]{:S(2)}) collective-permute-start(f32[2,128,512]{2,1,0:T(8,128)S(1)} %get-tuple-element.51), channel_id=1, source_target_pairs={{0,32},{32,0},{64,96},{96,64},{128,160},{160,128},{192,224},{224,1... | collective-permute-start | bytes 1572872 | tf_op jit(solution)/shard_map/ppermute | solution.py:229
  49.3 6.9 %collective-permute-start.17 = (bf16[128,256]{1,0:T(8,128)(2,1)S(1)}, bf16[128,256]{1,0:T(8,128)(2,1)S(1)}, u32[]{:S(2)}, u32[]{:S(2)}) collective-permute-start(bf16[128,256]{1,0:T(8,128)(2,1)S(1)} %fusion), channel_id=1, source_target_pairs={{64,0},{96,32},{128,64},{160,96},{192,128},{224,160},{65,1},{97,33... | collective-permute-start | bytes 196616 | tf_op jit(solution)/shard_map/ppermute | solution.py:235
  52.3 16.6 %collective-permute-start.12 = (bf16[128,256]{1,0:T(8,128)(2,1)S(1)}, bf16[128,256]{1,0:T(8,128)(2,1)S(1)}, u32[]{:S(2)}, u32[]{:S(2)}) collective-permute-start(bf16[128,256]{1,0:T(8,128)(2,1)S(1)} %get-tuple-element.59), channel_id=1, source_target_pairs={{192,0},{224,32},{193,1},{225,33},{194,2},{226,34},{195,3},{227,35... | collective-permute-start | bytes 196616 | tf_op jit(solution)/shard_map/ppermute | solution.py:235
  53.6 16.7 %collective-permute-start.13 = (bf16[128,256]{1,0:T(8,128)(2,1)S(1)}, bf16[128,256]{1,0:T(8,128)(2,1)S(1)}, u32[]{:S(2)}, u32[]{:S(2)}) collective-permute-start(bf16[128,256]{1,0:T(8,128)(2,1)S(1)} %get-tuple-element.60), channel_id=1, source_target_pairs={{128,0},{160,32},{192,64},{224,96},{129,1},{161,33},{193,65},{225,... | collective-permute-start | bytes 196616 | tf_op jit(solution)/shard_map/ppermute | solution.py:235
